TPU v7x, 32 devices: a whole 2x2x4 slice. The times are simulated.
32 devices in a mesh: lon: 8 (over z, core), lat: 4 (over y, x).
Axes of the slice: x: 2, y: 2, z: 4, core: 2. Of those that a mesh axis runs over, the one named last changes fastest.
Arguments:
- height: float32 [1, 1152, 4096], P(None, 'lat', 'lon'), may hold values from -6 to 6
- response: float32 [640], replicated, may hold values from 0.25 to 4
Outputs:
- loading: float32 [1, 1152, 4096], P(None, 'lat', 'lon')
All inputs are finite; a program needn't handle non-finite values.
Results may differ from a plain program's by a relative error of at most 0.00085.
Values sent between devices are 32-bit elements; how exact they have to be, the bound alone decides.
A program may use at most 64 MiB of HBM per device.

v0:
```python
import jax
import jax.numpy as jnp
from jax import lax
from jax.sharding import PartitionSpec as P

NLAT = 1152
NLON = 4096
MODES = 640


block_degrees = 64
rescale_every = 8
highest = lax.Precision.HIGHEST


def colatitude_parts(latitudes):
    colatitude = (latitudes.astype(jnp.float32) + 0.5) * (jnp.pi / NLAT)
    sines = jnp.sin(colatitude)
    return (jnp.cos(colatitude), sines, sines * (jnp.pi / NLAT))


def legendre_sweep(cosines, sines, orders, consume, initial):
    order_float = orders.astype(jnp.float32)
    log_start = 0.5 * (
        lax.lgamma(order_float + 1.5)
        - lax.lgamma(order_float + 1.0)
        - lax.lgamma(jnp.full_like(order_float, 1.5))
    ) - 0.5 * jnp.log(4.0 * jnp.pi)
    log_scale = log_start[:, None] + order_float[:, None] * jnp.log(sines)[None, :]
    zero_field = jnp.zeros(log_scale.shape, jnp.float32)

    def one_block(block_index, carried):
        earlier, latest, log_scale, running = carried
        first_degree = (block_index * block_degrees).astype(jnp.int32)
        factor = jnp.exp(log_scale)
        layers = []
        for offset in range(block_degrees):
            degree = first_degree + offset
            started = degree > orders
            starting = degree == orders
            degree_float = degree.astype(jnp.float32)
            lower_float = degree_float - 1.0
            square_gap = jnp.where(
                started, degree_float * degree_float - order_float * order_float, 1.0
            )
            growth = jnp.sqrt(
                jnp.where(started, (4.0 * degree_float * degree_float - 1.0) / square_gap, 0.0)
            )
            damping = jnp.sqrt(
                jnp.where(
                    started,
                    (lower_float * lower_float - order_float * order_float)
                    / jnp.maximum(4.0 * lower_float * lower_float - 1.0, 1.0),
                    0.0,
                )
            )
            current = jnp.where(
                starting[:, None],
                1.0,
                growth[:, None] * (cosines[None, :] * latest - damping[:, None] * earlier),
            )
            layers.append(current * factor)
            earlier, latest = (latest, current)
            if (offset + 1) % rescale_every == 0:
                largest = jnp.maximum(jnp.maximum(jnp.abs(earlier), jnp.abs(latest)), 1.0)
                earlier = earlier / largest
                latest = latest / largest
                log_scale = log_scale + jnp.log(largest)
                factor = jnp.exp(log_scale)
        legendre = jnp.stack(layers)
        return (earlier, latest, log_scale, consume(running, legendre, first_degree))

    carried = (zero_field, zero_field, log_scale, initial)
    carried = lax.fori_loop(0, MODES // block_degrees, one_block, carried)
    return carried[3]


def analyse(spectrum, latitudes, orders):
    cosines, sines, weights = colatitude_parts(latitudes)
    weighted = spectrum * weights

    def consume(coefficients, legendre, first_degree):
        block_terms = jnp.einsum("lmj,mcfj->lmcf", legendre, weighted, precision=highest)
        return lax.dynamic_update_slice_in_dim(coefficients, block_terms, first_degree, 0)

    initial = jnp.zeros((MODES,) + spectrum.shape[:3], jnp.float32)
    return legendre_sweep(cosines, sines, orders, consume, initial)


def synthesise(scaled, latitudes, orders):
    cosines, sines = colatitude_parts(latitudes)[:2]

    def consume(running, legendre, first_degree):
        scaled_block = lax.dynamic_slice_in_dim(scaled, first_degree, block_degrees, 0)
        return running + jnp.einsum("lmj,lmcf->mcfj", legendre, scaled_block, precision=highest)

    initial = jnp.zeros(scaled.shape[1:] + (latitudes.shape[0],), jnp.float32)
    return legendre_sweep(cosines, sines, orders, consume, initial)


def angle_table(wavenumbers, longitudes):
    product = wavenumbers[:, None] * longitudes[None, :] % NLON
    return product.astype(jnp.float32) * (2.0 * jnp.pi / NLON)


def forward_terms(field, wavenumbers, longitudes):
    angles = angle_table(wavenumbers, longitudes)
    spacing = 2.0 * jnp.pi / NLON
    real_part = jnp.einsum("mk,fjk->mfj", jnp.cos(angles) * spacing, field, precision=highest)
    imag_part = -jnp.einsum("mk,fjk->mfj", jnp.sin(angles) * spacing, field, precision=highest)
    return jnp.stack([real_part, imag_part], axis=1)


def inverse_terms(spectral_parts, wavenumbers, longitudes):
    angles = angle_table(wavenumbers, longitudes)
    weight = jnp.where(wavenumbers == 0, 1.0, 2.0)[:, None]
    real_part = jnp.einsum(
        "mk,mfj->fjk", jnp.cos(angles) * weight, spectral_parts[:, 0], precision=highest
    )
    imag_part = jnp.einsum(
        "mk,mfj->fjk", jnp.sin(angles) * weight, spectral_parts[:, 1], precision=highest
    )
    return real_part - imag_part


def shards(height, response):
    fields, band_rows, lon_cells = height.shape
    lon_count = lax.axis_size("lon")
    lat_count = lax.axis_size("lat")
    lon_index = lax.axis_index("lon")
    lat_index = lax.axis_index("lat")
    local_modes = MODES // lon_count
    longitudes = lon_index * lon_cells + jnp.arange(lon_cells, dtype=jnp.int32)
    wavenumbers = jnp.arange(lax.axis_size("lon") * local_modes, dtype=jnp.int32)
    spectrum = lax.psum_scatter(
        forward_terms(height, wavenumbers, longitudes), "lon", scatter_dimension=0, tiled=True
    )
    column_modes = local_modes // lat_count
    columns = lax.all_to_all(spectrum, "lat", split_axis=0, concat_axis=3, tiled=True)
    all_latitudes = jnp.arange(NLAT, dtype=jnp.int32)
    column_orders = (
        lon_index * local_modes
        + lat_index * column_modes
        + jnp.arange(column_modes, dtype=jnp.int32)
    )
    coefficients = analyse(columns, all_latitudes, column_orders)
    scaled = coefficients * response[:, None, None, None]
    column_synthesis = synthesise(scaled, all_latitudes, column_orders)
    synthesis = lax.all_to_all(column_synthesis, "lat", split_axis=3, concat_axis=0, tiled=True)
    shard_piece = lax.all_gather(synthesis, "lon", axis=0, tiled=True)
    wavenumbers = jnp.arange(shard_piece.shape[0], dtype=jnp.int32)
    return inverse_terms(shard_piece, wavenumbers, longitudes)


def solution(mesh):
    placed = (P(None, "lat", "lon"), P())
    return jax.shard_map(
        shards, mesh=mesh, in_specs=placed, out_specs=P(None, "lat", "lon"), check_vma=False
    )
```

profile of v0, /device:TPU:0, one launch (start us, length us, event | category | flops | bytes accessed | tf_op | source)
XLA Modules:
  0.0 1537.3 jit_solution(1907798716013058885)
XLA Ops:
  26.0 64.9 %all-reduce.3.cloned.1.call-done = f32[640,2,1,288]{3,1,2,0:T(2,128)} async-done(((f32[640,2,1,288]{3,1,2,0:T(2,128)}), f32[640,2,1,288]{3,1,2,0:T(2,128)}) %all-reduce.3.cloned.1.call-update) | async-done | bytes 1474576
  103.3 721.8 %while.52 = (s32[]{:T(128)}, f32[20,1152]{1,0:T(8,128)S(1)}, f32[20,1152]{1,0:T(8,128)S(1)}, f32[20,1152]{1,0:T(8,128)S(1)}, f32[640,20,2,1]{0,2,1,3:T(2,128)}, ...) while((s32[]{:T(128)}, f32[20,1152]{1,0:T(8,128)S(1)}, ...), condition=%wide.region_2.3_spmd.clone.clone.clone.clone, body=%wide.region_1.2_spmd.clone.clone.clone.clone.sunk | while | flops 47715584 | bytes 46390420 | solution.py:74
  140.7 22.6 %stack.1967 = f32[64,20,1152]{2,0,1:T(8,128)} concatenate(f32[1,20,1152]{2,0,1:T(1,128)} %copy.785, f32[1,20,1152]{2,0,1:T(1,128)} %copy.786, f32[1,20,1152]{2,0,1:T(1,128)} %copy.787, f32[1,20,1152]{2,0,1:T(1,128)} %copy.788, f32[1,20,1152]{2,0,1:T(1,128)} %copy.789, f32[1,20,1152]{2,0,1:T(1,128)} %copy.790, f32[1,20,1152]{2,0,1:T(1,128)} %copy.791, f32[1,20,1152]{2,0,1:T(1,128)} %copy.792, ...), dimensions={0} | concatenate | bytes 11796480 | tf_op jit(solution)/shard_map/while/body/eval_jaxpr/stack | solution.py:70
  210.1 22.6 %stack.1967 = f32[64,20,1152]{2,0,1:T(8,128)} concatenate(f32[1,20,1152]{2,0,1:T(1,128)} %copy.785, f32[1,20,1152]{2,0,1:T(1,128)} %copy.786, f32[1,20,1152]{2,0,1:T(1,128)} %copy.787, f32[1,20,1152]{2,0,1:T(1,128)} %copy.788, f32[1,20,1152]{2,0,1:T(1,128)} %copy.789, f32[1,20,1152]{2,0,1:T(1,128)} %copy.790, f32[1,20,1152]{2,0,1:T(1,128)} %copy.791, f32[1,20,1152]{2,0,1:T(1,128)} %copy.792, ...), dimensions={0} | concatenate | bytes 11796480 | tf_op jit(solution)/shard_map/while/body/eval_jaxpr/stack | solution.py:70
  282.3 22.6 %stack.1967 = f32[64,20,1152]{2,0,1:T(8,128)} concatenate(f32[1,20,1152]{2,0,1:T(1,128)} %copy.785, f32[1,20,1152]{2,0,1:T(1,128)} %copy.786, f32[1,20,1152]{2,0,1:T(1,128)} %copy.787, f32[1,20,1152]{2,0,1:T(1,128)} %copy.788, f32[1,20,1152]{2,0,1:T(1,128)} %copy.789, f32[1,20,1152]{2,0,1:T(1,128)} %copy.790, f32[1,20,1152]{2,0,1:T(1,128)} %copy.791, f32[1,20,1152]{2,0,1:T(1,128)} %copy.792, ...), dimensions={0} | concatenate | bytes 11796480 | tf_op jit(solution)/shard_map/while/body/eval_jaxpr/stack | solution.py:70
  351.7 22.6 %stack.1967 = f32[64,20,1152]{2,0,1:T(8,128)} concatenate(f32[1,20,1152]{2,0,1:T(1,128)} %copy.785, f32[1,20,1152]{2,0,1:T(1,128)} %copy.786, f32[1,20,1152]{2,0,1:T(1,128)} %copy.787, f32[1,20,1152]{2,0,1:T(1,128)} %copy.788, f32[1,20,1152]{2,0,1:T(1,128)} %copy.789, f32[1,20,1152]{2,0,1:T(1,128)} %copy.790, f32[1,20,1152]{2,0,1:T(1,128)} %copy.791, f32[1,20,1152]{2,0,1:T(1,128)} %copy.792, ...), dimensions={0} | concatenate | bytes 11796480 | tf_op jit(solution)/shard_map/while/body/eval_jaxpr/stack | solution.py:70
  423.9 22.6 %stack.1967 = f32[64,20,1152]{2,0,1:T(8,128)} concatenate(f32[1,20,1152]{2,0,1:T(1,128)} %copy.785, f32[1,20,1152]{2,0,1:T(1,128)} %copy.786, f32[1,20,1152]{2,0,1:T(1,128)} %copy.787, f32[1,20,1152]{2,0,1:T(1,128)} %copy.788, f32[1,20,1152]{2,0,1:T(1,128)} %copy.789, f32[1,20,1152]{2,0,1:T(1,128)} %copy.790, f32[1,20,1152]{2,0,1:T(1,128)} %copy.791, f32[1,20,1152]{2,0,1:T(1,128)} %copy.792, ...), dimensions={0} | concatenate | bytes 11796480 | tf_op jit(solution)/shard_map/while/body/eval_jaxpr/stack | solution.py:70
  493.3 22.6 %stack.1967 = f32[64,20,1152]{2,0,1:T(8,128)} concatenate(f32[1,20,1152]{2,0,1:T(1,128)} %copy.785, f32[1,20,1152]{2,0,1:T(1,128)} %copy.786, f32[1,20,1152]{2,0,1:T(1,128)} %copy.787, f32[1,20,1152]{2,0,1:T(1,128)} %copy.788, f32[1,20,1152]{2,0,1:T(1,128)} %copy.789, f32[1,20,1152]{2,0,1:T(1,128)} %copy.790, f32[1,20,1152]{2,0,1:T(1,128)} %copy.791, f32[1,20,1152]{2,0,1:T(1,128)} %copy.792, ...), dimensions={0} | concatenate | bytes 11796480 | tf_op jit(solution)/shard_map/while/body/eval_jaxpr/stack | solution.py:70
  565.4 22.6 %stack.1967 = f32[64,20,1152]{2,0,1:T(8,128)} concatenate(f32[1,20,1152]{2,0,1:T(1,128)} %copy.785, f32[1,20,1152]{2,0,1:T(1,128)} %copy.786, f32[1,20,1152]{2,0,1:T(1,128)} %copy.787, f32[1,20,1152]{2,0,1:T(1,128)} %copy.788, f32[1,20,1152]{2,0,1:T(1,128)} %copy.789, f32[1,20,1152]{2,0,1:T(1,128)} %copy.790, f32[1,20,1152]{2,0,1:T(1,128)} %copy.791, f32[1,20,1152]{2,0,1:T(1,128)} %copy.792, ...), dimensions={0} | concatenate | bytes 11796480 | tf_op jit(solution)/shard_map/while/body/eval_jaxpr/stack | solution.py:70
  634.9 22.6 %stack.1967 = f32[64,20,1152]{2,0,1:T(8,128)} concatenate(f32[1,20,1152]{2,0,1:T(1,128)} %copy.785, f32[1,20,1152]{2,0,1:T(1,128)} %copy.786, f32[1,20,1152]{2,0,1:T(1,128)} %copy.787, f32[1,20,1152]{2,0,1:T(1,128)} %copy.788, f32[1,20,1152]{2,0,1:T(1,128)} %copy.789, f32[1,20,1152]{2,0,1:T(1,128)} %copy.790, f32[1,20,1152]{2,0,1:T(1,128)} %copy.791, f32[1,20,1152]{2,0,1:T(1,128)} %copy.792, ...), dimensions={0} | concatenate | bytes 11796480 | tf_op jit(solution)/shard_map/while/body/eval_jaxpr/stack | solution.py:70
  707.0 22.6 %stack.1967 = f32[64,20,1152]{2,0,1:T(8,128)} concatenate(f32[1,20,1152]{2,0,1:T(1,128)} %copy.785, f32[1,20,1152]{2,0,1:T(1,128)} %copy.786, f32[1,20,1152]{2,0,1:T(1,128)} %copy.787, f32[1,20,1152]{2,0,1:T(1,128)} %copy.788, f32[1,20,1152]{2,0,1:T(1,128)} %copy.789, f32[1,20,1152]{2,0,1:T(1,128)} %copy.790, f32[1,20,1152]{2,0,1:T(1,128)} %copy.791, f32[1,20,1152]{2,0,1:T(1,128)} %copy.792, ...), dimensions={0} | concatenate | bytes 11796480 | tf_op jit(solution)/shard_map/while/body/eval_jaxpr/stack | solution.py:70
  776.3 22.6 %stack.1967 = f32[64,20,1152]{2,0,1:T(8,128)} concatenate(f32[1,20,1152]{2,0,1:T(1,128)} %copy.785, f32[1,20,1152]{2,0,1:T(1,128)} %copy.786, f32[1,20,1152]{2,0,1:T(1,128)} %copy.787, f32[1,20,1152]{2,0,1:T(1,128)} %copy.788, f32[1,20,1152]{2,0,1:T(1,128)} %copy.789, f32[1,20,1152]{2,0,1:T(1,128)} %copy.790, f32[1,20,1152]{2,0,1:T(1,128)} %copy.791, f32[1,20,1152]{2,0,1:T(1,128)} %copy.792, ...), dimensions={0} | concatenate | bytes 11796480 | tf_op jit(solution)/shard_map/while/body/eval_jaxpr/stack | solution.py:70
  826.7 640.3 %while.53 = (s32[]{:T(128)}, f32[20,1152]{1,0:T(8,128)S(1)}, f32[20,1152]{1,0:T(8,128)S(1)}, f32[20,1152]{1,0:T(8,128)S(1)}, f32[20,2,1,1152]{3,1,0,2:T(2,128)},...) while((s32[]{:T(128)}, f32[20,1152]{1,0:T(8,128)S(1)}, ...), condition=%wide.region_4.5_spmd.clone.clone.clone.clone, body=%wide.region_3.4_spmd.clone.clone.clone.clone.sunk | while | flops 47807748 | bytes 46559628 | solution.py:74
  862.5 21.7 %stack.1969 = f32[64,20,1152]{2,0,1:T(8,128)} concatenate(f32[1,20,1152]{2,0,1:T(1,128)} %copy.848, f32[1,20,1152]{2,0,1:T(1,128)} %copy.849, f32[1,20,1152]{2,0,1:T(1,128)} %copy.850, f32[1,20,1152]{2,0,1:T(1,128)} %copy.851, f32[1,20,1152]{2,0,1:T(1,128)} %copy.852, f32[1,20,1152]{2,0,1:T(1,128)} %copy.853, f32[1,20,1152]{2,0,1:T(1,128)} %copy.854, f32[1,20,1152]{2,0,1:T(1,128)} %copy.855, ...), dimensions={0} | concatenate | bytes 11796480 | tf_op jit(solution)/shard_map/while/body/eval_jaxpr/stack | solution.py:70
  926.5 21.7 %stack.1969 = f32[64,20,1152]{2,0,1:T(8,128)} concatenate(f32[1,20,1152]{2,0,1:T(1,128)} %copy.848, f32[1,20,1152]{2,0,1:T(1,128)} %copy.849, f32[1,20,1152]{2,0,1:T(1,128)} %copy.850, f32[1,20,1152]{2,0,1:T(1,128)} %copy.851, f32[1,20,1152]{2,0,1:T(1,128)} %copy.852, f32[1,20,1152]{2,0,1:T(1,128)} %copy.853, f32[1,20,1152]{2,0,1:T(1,128)} %copy.854, f32[1,20,1152]{2,0,1:T(1,128)} %copy.855, ...), dimensions={0} | concatenate | bytes 11796480 | tf_op jit(solution)/shard_map/while/body/eval_jaxpr/stack | solution.py:70
  990.5 21.7 %stack.1969 = f32[64,20,1152]{2,0,1:T(8,128)} concatenate(f32[1,20,1152]{2,0,1:T(1,128)} %copy.848, f32[1,20,1152]{2,0,1:T(1,128)} %copy.849, f32[1,20,1152]{2,0,1:T(1,128)} %copy.850, f32[1,20,1152]{2,0,1:T(1,128)} %copy.851, f32[1,20,1152]{2,0,1:T(1,128)} %copy.852, f32[1,20,1152]{2,0,1:T(1,128)} %copy.853, f32[1,20,1152]{2,0,1:T(1,128)} %copy.854, f32[1,20,1152]{2,0,1:T(1,128)} %copy.855, ...), dimensions={0} | concatenate | bytes 11796480 | tf_op jit(solution)/shard_map/while/body/eval_jaxpr/stack | solution.py:70
  1054.5 21.7 %stack.1969 = f32[64,20,1152]{2,0,1:T(8,128)} concatenate(f32[1,20,1152]{2,0,1:T(1,128)} %copy.848, f32[1,20,1152]{2,0,1:T(1,128)} %copy.849, f32[1,20,1152]{2,0,1:T(1,128)} %copy.850, f32[1,20,1152]{2,0,1:T(1,128)} %copy.851, f32[1,20,1152]{2,0,1:T(1,128)} %copy.852, f32[1,20,1152]{2,0,1:T(1,128)} %copy.853, f32[1,20,1152]{2,0,1:T(1,128)} %copy.854, f32[1,20,1152]{2,0,1:T(1,128)} %copy.855, ...), dimensions={0} | concatenate | bytes 11796480 | tf_op jit(solution)/shard_map/while/body/eval_jaxpr/stack | solution.py:70
  1118.5 21.7 %stack.1969 = f32[64,20,1152]{2,0,1:T(8,128)} concatenate(f32[1,20,1152]{2,0,1:T(1,128)} %copy.848, f32[1,20,1152]{2,0,1:T(1,128)} %copy.849, f32[1,20,1152]{2,0,1:T(1,128)} %copy.850, f32[1,20,1152]{2,0,1:T(1,128)} %copy.851, f32[1,20,1152]{2,0,1:T(1,128)} %copy.852, f32[1,20,1152]{2,0,1:T(1,128)} %copy.853, f32[1,20,1152]{2,0,1:T(1,128)} %copy.854, f32[1,20,1152]{2,0,1:T(1,128)} %copy.855, ...), dimensions={0} | concatenate | bytes 11796480 | tf_op jit(solution)/shard_map/while/body/eval_jaxpr/stack | solution.py:70
  1182.5 21.7 %stack.1969 = f32[64,20,1152]{2,0,1:T(8,128)} concatenate(f32[1,20,1152]{2,0,1:T(1,128)} %copy.848, f32[1,20,1152]{2,0,1:T(1,128)} %copy.849, f32[1,20,1152]{2,0,1:T(1,128)} %copy.850, f32[1,20,1152]{2,0,1:T(1,128)} %copy.851, f32[1,20,1152]{2,0,1:T(1,128)} %copy.852, f32[1,20,1152]{2,0,1:T(1,128)} %copy.853, f32[1,20,1152]{2,0,1:T(1,128)} %copy.854, f32[1,20,1152]{2,0,1:T(1,128)} %copy.855, ...), dimensions={0} | concatenate | bytes 11796480 | tf_op jit(solution)/shard_map/while/body/eval_jaxpr/stack | solution.py:70
  1246.5 21.7 %stack.1969 = f32[64,20,1152]{2,0,1:T(8,128)} concatenate(f32[1,20,1152]{2,0,1:T(1,128)} %copy.848, f32[1,20,1152]{2,0,1:T(1,128)} %copy.849, f32[1,20,1152]{2,0,1:T(1,128)} %copy.850, f32[1,20,1152]{2,0,1:T(1,128)} %copy.851, f32[1,20,1152]{2,0,1:T(1,128)} %copy.852, f32[1,20,1152]{2,0,1:T(1,128)} %copy.853, f32[1,20,1152]{2,0,1:T(1,128)} %copy.854, f32[1,20,1152]{2,0,1:T(1,128)} %copy.855, ...), dimensions={0} | concatenate | bytes 11796480 | tf_op jit(solution)/shard_map/while/body/eval_jaxpr/stack | solution.py:70
  1310.5 21.7 %stack.1969 = f32[64,20,1152]{2,0,1:T(8,128)} concatenate(f32[1,20,1152]{2,0,1:T(1,128)} %copy.848, f32[1,20,1152]{2,0,1:T(1,128)} %copy.849, f32[1,20,1152]{2,0,1:T(1,128)} %copy.850, f32[1,20,1152]{2,0,1:T(1,128)} %copy.851, f32[1,20,1152]{2,0,1:T(1,128)} %copy.852, f32[1,20,1152]{2,0,1:T(1,128)} %copy.853, f32[1,20,1152]{2,0,1:T(1,128)} %copy.854, f32[1,20,1152]{2,0,1:T(1,128)} %copy.855, ...), dimensions={0} | concatenate | bytes 11796480 | tf_op jit(solution)/shard_map/while/body/eval_jaxpr/stack | solution.py:70
  1374.5 21.7 %stack.1969 = f32[64,20,1152]{2,0,1:T(8,128)} concatenate(f32[1,20,1152]{2,0,1:T(1,128)} %copy.848, f32[1,20,1152]{2,0,1:T(1,128)} %copy.849, f32[1,20,1152]{2,0,1:T(1,128)} %copy.850, f32[1,20,1152]{2,0,1:T(1,128)} %copy.851, f32[1,20,1152]{2,0,1:T(1,128)} %copy.852, f32[1,20,1152]{2,0,1:T(1,128)} %copy.853, f32[1,20,1152]{2,0,1:T(1,128)} %copy.854, f32[1,20,1152]{2,0,1:T(1,128)} %copy.855, ...), dimensions={0} | concatenate | bytes 11796480 | tf_op jit(solution)/shard_map/while/body/eval_jaxpr/stack | solution.py:70
  1438.5 21.7 %stack.1969 = f32[64,20,1152]{2,0,1:T(8,128)} concatenate(f32[1,20,1152]{2,0,1:T(1,128)} %copy.848, f32[1,20,1152]{2,0,1:T(1,128)} %copy.849, f32[1,20,1152]{2,0,1:T(1,128)} %copy.850, f32[1,20,1152]{2,0,1:T(1,128)} %copy.851, f32[1,20,1152]{2,0,1:T(1,128)} %copy.852, f32[1,20,1152]{2,0,1:T(1,128)} %copy.853, f32[1,20,1152]{2,0,1:T(1,128)} %copy.854, f32[1,20,1152]{2,0,1:T(1,128)} %copy.855, ...), dimensions={0} | concatenate | bytes 11796480 | tf_op jit(solution)/shard_map/while/body/eval_jaxpr/stack | solution.py:70
  1483.7 26.1 %all-gather.2.cloned.1.call-done = f32[640,2,1,288]{3,1,2,0:T(2,128)} async-done(((f32[80,2,1,288]{3,1,2,0:T(2,128)}), f32[640,2,1,288]{3,1,2,0:T(2,128)}) %all-gather.2.cloned.1.call-update) | async-done | bytes 1474576 | tf_op jit(solution)/shard_map/all_gather | solution.py:150
  (5062 shorter events, 924.8 us)
Async XLA Ops:
  6.5 84.4 %all-reduce.3.cloned.1.call-start = ((), (), s32[]{:S(2)}) async-start(), calls=%async_computation.3 | async-start | bytes 3932160
  92.6 9.0 all-to-all-start
  96.3 1413.5 %all-gather.2.cloned.1.call-start = ((), (), s32[]{:S(2)}) async-start(), calls=%async_computation.2 | async-start | bytes 2211840 | tf_op jit(solution)/shard_map/all_gather | solution.py:150
  103.6 7.4 copy-start.56
  173.0 7.4 copy-start.56
  245.2 7.4 copy-start.56
  314.6 7.4 copy-start.56
  386.8 7.4 copy-start.56
  456.2 7.4 copy-start.56
  528.3 7.4 copy-start.56
  597.8 7.4 copy-start.56
  669.9 7.4 copy-start.56
  739.2 7.4 copy-start.56
  826.7 7.4 copy-start.58
  890.7 7.4 copy-start.58
  954.7 7.4 copy-start.58
  1018.7 7.4 copy-start.58
  1082.7 7.4 copy-start.58
  1146.7 7.4 copy-start.58
  1210.7 7.4 copy-start.58
  1274.7 7.4 copy-start.58
  1338.7 7.4 copy-start.58
  1402.7 7.4 copy-start.58
  1523.0 7.3 copy-start.1
  (764 other events, 3714.3 us)
Sparse Core Ops, SparseCore 0:
  24.1 66.7 all-reduce.2
  1483.8 25.9 all-gather.1
where the time goes:
time: 1560 us; the launch traced here: 1540 us
  local copies, waits for them, and re-layouts  1040 us (67%)
  matrix products  173 us (11%)
  other arithmetic  140 us (9%)
  waiting for transfers between devices  96.1 us (6%)
  loops' own time  63.9 us (4%)
    another operation x1300, local copies, waits for them, and re-layouts, one_block(): legendre = jnp.stack(layers)  984 us
    mul x20, other arithmetic, one_block(): layers.append(current * factor)  84.2 us
    dot_general x10, matrix products, consume(): jnp.einsum('lmj,mcfj->lmcf', legendre, weighted, precision=highest)  81.2 us
    unnamed x3, waiting for transfers between devices  64.9 us
    dot_general x10, matrix products, consume(): jnp.einsum('lmj,lmcf->mcfj', legendre, scaled_block, precision=highest)  64.4 us
    another operation x2, loops' own time, legendre_sweep(): carried = lax.fori_loop(0, MODES // block_degrees, one_block, carried)  63.9 us

commit v1 on v0

v1 whole, which is shorter than its diff:
```python
import functools
import math

import jax
import jax.numpy as jnp
import numpy as np
from jax import lax
from jax.experimental import pallas as pl
from jax.experimental.pallas import tpu as pltpu
from jax.sharding import PartitionSpec as P

STEPS = 16
LANES = 128
RESCALE = 2.0 ** -64
THRESHOLD = 2.0 ** 32
high = lax.Precision.HIGH


def mode_order(modes, devices):
    count = modes // devices
    order = np.zeros((devices, count), np.int64)
    device = np.arange(devices)
    for slot in range((count + 1) // 2):
        order[:, slot] = slot * devices + device
        if slot != count - 1 - slot:
            order[:, count - 1 - slot] = modes - 1 - order[:, slot]
    return order


def sweep_kernel(resets, table, log_start, cosines, weights, out_first, out_second,
                 earlier, latest, log_scale, current_weights, sums):
    blocks = table.shape[0]
    groups = table.shape[1] // 8
    earlier[...] = jnp.zeros_like(earlier)
    latest[...] = jnp.zeros_like(latest)
    log_scale[...] = log_start[0]
    current_weights[...] = weights[0]
    sums[...] = jnp.zeros_like(sums)
    out_first[...] = jnp.zeros_like(out_first)

    def one_block(block, carry):
        @pl.when(resets[block] > 0)
        def _():
            switching = table[block][:, 48:49] > 0.5
            earlier[...] = jnp.where(switching, 0.0, earlier[...])
            latest[...] = jnp.where(switching, 0.0, latest[...])
            log_scale[...] = jnp.where(switching, log_start[1], log_scale[...])
            for parity in range(2):
                for part in range(2):
                    index = (parity, part)
                    current_weights[index] = jnp.where(
                        switching, weights[(1,) + index], current_weights[index]
                    )
                    out_first[index] = jnp.where(switching, sums[index], out_first[index])
                    sums[index] = jnp.where(switching, 0.0, sums[index])

        x = cosines[...]
        for group in range(groups):
            rows = pl.ds(group * 8, 8)
            columns = table[block, rows, :]
            before = earlier[rows, :]
            last = latest[rows, :]
            scale = log_scale[rows, :]
            factor = jnp.exp(scale)
            totals = [[None, None], [None, None]]
            for step in range(STEPS):
                growth = columns[:, step:step + 1]
                ratio = columns[:, STEPS + step:STEPS + step + 1]
                answer = columns[:, 2 * STEPS + step:2 * STEPS + step + 1]
                current = growth * (x * last) - ratio * before
                if step == 0:
                    current = current + columns[:, 49:50]
                before, last = last, current
                legendre = current * factor
                parity = step % 2
                for part in range(2):
                    product = legendre * current_weights[parity, part, rows, :]
                    coefficient = jnp.sum(product, axis=1, keepdims=True) * answer
                    term = legendre * coefficient
                    total = totals[parity][part]
                    totals[parity][part] = term if total is None else total + term
            for parity in range(2):
                for part in range(2):
                    sums[parity, part, rows, :] += totals[parity][part]
            large = jnp.maximum(jnp.abs(before), jnp.abs(last)) > THRESHOLD
            shrink = jnp.where(large, RESCALE, 1.0)
            earlier[rows, :] = before * shrink
            latest[rows, :] = last * shrink
            log_scale[rows, :] = scale + jnp.where(large, 64.0 * math.log(2.0), 0.0)
        return carry

    lax.fori_loop(0, blocks, one_block, 0)
    out_second[...] = sums[...]


def sweep(columns, response, device, devices, modes, cells):
    parts, slots, rows = columns.shape
    half = rows // 2
    padded_half = -(-half // LANES) * LANES
    chains = (slots + 1) // 2
    padded_chains = -(-chains // 8) * 8
    blocks = modes // STEPS + 1
    total_steps = blocks * STEPS

    chain = np.where(np.arange(padded_chains) < chains, np.arange(padded_chains), 0)
    first = jnp.asarray(chain * devices, jnp.int32) + device
    second = modes - 1 - first
    switch = ((modes - first + STEPS - 1) // STEPS) * STEPS
    step = jnp.arange(total_steps, dtype=jnp.int32)[:, None]
    in_first = step < switch[None, :]
    degree = jnp.where(in_first, first + step, second + step - switch)
    order = jnp.where(in_first, first, second)
    degree_float = degree.astype(jnp.float32)
    order_float = order.astype(jnp.float32)
    lower = degree_float - 1.0
    started = degree > order
    gap = jnp.where(started, degree_float * degree_float - order_float * order_float, 1.0)
    growth = jnp.where(
        started, jnp.sqrt((4.0 * degree_float * degree_float - 1.0) / gap), 0.0
    )
    damping = jnp.sqrt(
        jnp.where(
            started,
            (lower * lower - order_float * order_float)
            / jnp.maximum(4.0 * lower * lower - 1.0, 1.0),
            0.0,
        )
    )
    padded_response = jnp.pad(response, (STEPS, total_steps + STEPS))
    from_device = lax.dynamic_slice_in_dim(
        padded_response, STEPS + device, modes + STEPS
    )
    from_device = jnp.pad(from_device, (0, total_steps + (padded_chains + 1) * devices))
    first_response = jnp.stack(
        [from_device[c * devices:c * devices + total_steps] for c in chain], axis=1
    )
    offset = modes - 1 - device - ((modes - device + STEPS - 1) // STEPS) * STEPS
    second_response = lax.dynamic_slice_in_dim(
        padded_response, STEPS + offset, total_steps
    )[:, None]
    answers = jnp.where(in_first, first_response, second_response)
    blocked = [
        part.reshape(blocks, STEPS, padded_chains)
        for part in (growth, growth * damping, answers)
    ]
    block_first = jnp.arange(blocks, dtype=jnp.int32)[:, None, None] * STEPS
    switching = block_first == switch[None, None, :]
    starting = jnp.logical_or(switching, block_first == 0)
    flags = [switching.astype(jnp.float32), starting.astype(jnp.float32)]
    table = jnp.concatenate(blocked + flags, axis=1).transpose(0, 2, 1)
    table = jnp.pad(table, ((0, 0), (0, 0), (0, LANES - table.shape[2])))
    resets = jnp.any(switching, axis=(1, 2)).astype(jnp.int32)

    colatitude = (np.arange(padded_half) + 0.5) * (math.pi / rows)
    colatitude = np.where(np.arange(padded_half) < half, colatitude, math.pi / 2)
    cosines = np.broadcast_to(np.cos(colatitude).astype(np.float32), (8, padded_half))
    log_sines = jnp.asarray(np.log(np.sin(colatitude)).astype(np.float32))
    log_norm = np.array([
        0.5 * (math.lgamma(m + 1.5) - math.lgamma(1.5) - math.lgamma(m + 1.0))
        - 0.5 * math.log(4.0 * math.pi)
        for m in range(modes)
    ])
    per_device = mode_order(modes, devices)
    chosen = per_device[:, chain]
    starts = np.stack([log_norm[chosen], log_norm[modes - 1 - chosen]], axis=1)
    starts = lax.dynamic_index_in_dim(
        jnp.asarray(starts.astype(np.float32)), device, 0, keepdims=False
    )
    orders = jnp.stack([first, second]).astype(jnp.float32)
    log_start = starts[:, :, None] + orders[:, :, None] * log_sines

    spacing = 2.0 * math.pi / cells
    area = np.sin(colatitude) * (math.pi / rows) * spacing
    area = jnp.asarray(area[:half].astype(np.float32))
    slot_orders = lax.dynamic_index_in_dim(
        jnp.asarray(per_device.astype(np.int32)), device, 0, keepdims=False
    )
    gain = jnp.where(slot_orders == 0, 1.0, 2.0)[None, :, None] * area
    north = columns[:, :, :half]
    south = columns[:, :, half:][:, :, ::-1]
    folded = jnp.stack([(north + south) * gain, (north - south) * gain])
    pad_chain = ((0, 0), (0, 0), (0, padded_chains - chains), (0, padded_half - half))
    weights = jnp.stack([
        jnp.pad(folded[:, :, :chains], pad_chain),
        jnp.pad(folded[:, :, ::-1][:, :, :chains], pad_chain),
    ])

    shape = (padded_chains, padded_half)
    sums_shape = (2, parts) + shape
    vmem = pl.BlockSpec(memory_space=pltpu.VMEM)
    first_sums, second_sums = pl.pallas_call(
        sweep_kernel,
        out_shape=[jax.ShapeDtypeStruct(sums_shape, jnp.float32)] * 2,
        in_specs=[pl.BlockSpec(memory_space=pltpu.SMEM)] + [vmem] * 4,
        out_specs=[vmem] * 2,
        scratch_shapes=[pltpu.VMEM(shape, jnp.float32)] * 3
        + [pltpu.VMEM(sums_shape, jnp.float32)] * 2,
        name="legendre_sweep",
    )(resets, table, log_start, jnp.asarray(cosines), weights)
    partners = slots - chains
    joined = jnp.concatenate(
        [first_sums[:, :, :chains, :half], second_sums[:, :, :partners, :half][:, :, ::-1]],
        axis=2,
    )
    north = joined[0] + joined[1]
    south = (joined[0] - joined[1])[:, :, ::-1]
    return jnp.concatenate([north, south], axis=2)


def shards(modes, height, response):
    fields, band_rows, lon_cells = height.shape
    lon_count = lax.axis_size("lon")
    lat_count = lax.axis_size("lat")
    lon_index = lax.axis_index("lon")
    lat_index = lax.axis_index("lat")
    devices = lon_count * lat_count
    slots = modes // devices
    cells = lon_count * lon_cells
    device = lon_index * lat_count + lat_index

    order = mode_order(modes, devices)
    local = np.arange(lon_cells)
    angles = (order[:, :, None] * local % cells) * (2.0 * math.pi / cells)
    cos_table = jnp.asarray(np.cos(angles).astype(np.float32))
    sin_table = jnp.asarray(np.sin(angles).astype(np.float32))
    turn = (jnp.asarray(order.astype(np.int32)) * (lon_index * lon_cells) % cells)
    turn = turn.astype(jnp.float32)[:, :, None] * (2.0 * math.pi / cells)
    cos_turn, sin_turn = jnp.cos(turn), jnp.sin(turn)
    table = jnp.stack(
        [
            cos_turn * cos_table - sin_turn * sin_table,
            -(sin_turn * cos_table + cos_turn * sin_table),
        ],
        axis=1,
    ).reshape(2 * modes, lon_cells)

    outputs = []
    for field in range(fields):
        partial = lax.dot_general(
            table, height[field], (((1,), (1,)), ((), ())), precision=high,
            preferred_element_type=jnp.float32,
        )
        spectrum = lax.psum_scatter(partial, "lon", scatter_dimension=0, tiled=True)
        columns = lax.all_to_all(spectrum, "lat", split_axis=0, concat_axis=1, tiled=True)
        columns = columns.reshape(2, slots, lat_count * band_rows)
        synthesis = sweep(columns, response, device, devices, modes, cells)
        synthesis = synthesis.reshape(2 * slots, lat_count * band_rows)
        bands = lax.all_to_all(synthesis, "lat", split_axis=1, concat_axis=0, tiled=True)
        gathered = lax.all_gather(bands, "lon", axis=0, tiled=True)
        outputs.append(lax.dot_general(
            gathered, table, (((0,), (0,)), ((), ())), precision=high,
            preferred_element_type=jnp.float32,
        ))
    return jnp.stack(outputs)


def solution(mesh):
    placed = (P(None, "lat", "lon"), P())

    def loading(height, response):
        body = functools.partial(shards, response.shape[0])
        return jax.shard_map(
            body, mesh=mesh, in_specs=placed, out_specs=P(None, "lat", "lon"), check_vma=False
        )(height, response)

    return loading
```

time: 1560 us -> 312 us (0.20); the launches traced: 1540 us -> 310 us
  local copies, waits for them, and re-layouts: 1040 us -> 31.4 us
  Pallas kernels: 0 us -> 179 us
  matrix products: 173 us -> 7.92 us
  other arithmetic: 140 us -> 16.8 us
  loops' own time: 63.9 us -> 0 us
  waiting for transfers between devices: 96.1 us -> 48.3 us
    another operation x1301 -> x13, local copies, waits for them, and re-layouts: 987 us -> 9.93 us  [the longest x11 9.28 us: sweep(): jnp.stack([from_device[c * devices:c * devices + total_steps] for c in ch...]
    pallas_call x0 -> x1, Pallas kernels: none -> 179 us  [sweep(): pl.pallas_call(sweep_kernel, out_shape=[jax.ShapeDtypeStruct(sums_shape,...]
    dot_general x24 -> x2, matrix products: 173 us -> 7.92 us  [the longest x1 4.44 us: shards(): lax.dot_general(gathered, table, (((0,), (0,)), ((), ())), precision=high...]
    mul x23 -> x3, other arithmetic: 86.6 us -> 2.38 us  [the longest x1 2.3 us: sweep(): growth * damping]
    unnamed x3 -> x2, waiting for transfers between devices: 64.9 us -> 0.03 us
    another operation x2 -> x0, loops' own time: 63.9 us -> none  [legendre_sweep(): carried = lax.fori_loop(0, MODES // block_degrees, one_block, carried)]
    dynamic_update_slice x10 -> x0, local copies, waits for them, and re-layouts: 28.8 us -> none  [consume(): lax.dynamic_update_slice_in_dim(coefficients, block_terms, first_degree, 0)]
    sqrt x1280 -> x0, other arithmetic: 21.6 us -> none  [the longest x640 11.8 us: one_block(): jnp.sqrt(jnp.where(started, (4.0 * degree_float * degree_float - 1.0) / s...]
where the time goes in v1:
time: 312 us; the launch traced here: 310 us
  Pallas kernels  179 us (57%)
  waiting for transfers between devices  48.3 us (15%)
  local copies, waits for them, and re-layouts  31.4 us (10%)
  other arithmetic  16.8 us (5%)
  between operations  13.6 us (4%)
  blocking collectives  8.74 us (3%)
  matrix products  7.92 us (3%)
  starting transfers between devices  3.82 us (1%)
    pallas_call x1, Pallas kernels, sweep(): pl.pallas_call(sweep_kernel, out_shape=[jax.ShapeDtypeStruct(sums_shape,...  179 us
    all_gather x1, waiting for transfers between devices, shards(): gathered = lax.all_gather(bands, 'lon', axis=0, tiled=True)  25.1 us
    reduce_scatter x1, waiting for transfers between devices, shards(): spectrum = lax.psum_scatter(partial, 'lon', scatter_dimension=0, tiled=True)  17.9 us
    another operation x11, local copies, waits for them, and re-layouts, sweep(): jnp.stack([from_device[c * devices:c * devices + total_steps] for c in ch...  9.28 us
    all_to_all x1, blocking collectives, shards(): lax.all_to_all(synthesis, 'lat', split_axis=1, concat_axis=0, tiled=True)  8.74 us
  transfers between devices with their start and end apart: 3, of which 3 were waited for; matrix products, arithmetic and copies ran while one was open for 6% of the time, Pallas kernels for 0%

profile of v1, /device:TPU:0, one launch (start us, length us, event | category | flops | bytes accessed | tf_op | source)
XLA Modules:
  0.0 310.0 jit_solution(10930270066488013068)
XLA Ops:
  6.5 0.9 fusion.25
  7.4 2.3 subtract_bitcast_fusion
  9.7 2.1 pad_maximum_fusion
  11.8 2.7 reshape.422
  14.5 3.5 %fusion = f32[1280,288]{1,0:T(8,128)} fusion(f32[1280,512]{1,0:T(8,128)S(1)} %reshape.422, f32[1,288,512]{2,1,0:T(8,128)S(1)} %copy-done), kind=kOutput, calls=%fused_computation.4 | convolution fusion | flops 1132462080 | bytes 4685824 | tf_op jit(solution)/shard_map/dot_general | solution.py:239
  27.1 1.1 fusion.18
  28.7 2.4 stack.88
  31.0 2.3 fusion.14
  33.4 1.9 concatenate.14
  38.7 17.9 %reduce-scatter.2.cloned.1.call-done = f32[160,288]{1,0:T(8,128)} async-done(((f32[1280,288]{1,0:T(8,128)}), f32[160,288]{1,0:T(8,128)}) %reduce-scatter.2.cloned.1.call-update) | async-done | bytes 184336 | tf_op jit(solution)/shard_map/reduce_scatter | solution.py:243
  56.6 3.8 %all-to-all-start = ((f32[4,40,288]{2,1,0:T(8,128)}), f32[4,40,288]{2,1,0:T(8,128)S(1)}, u32[]{:S(2)}, u32[]{:S(2)}) async-start(f32[4,40,288]{2,1,0:T(8,128)} %bitcast.49), calls=%async_computation.1 | async-start | bytes 491520 | tf_op jit(solution)/shard_map/all_to_all | solution.py:244
  60.5 5.2 %all-to-all-done = f32[4,40,288]{2,1,0:T(8,128)S(1)} async-done(((f32[4,40,288]{2,1,0:T(8,128)}), f32[4,40,288]{2,1,0:T(8,128)S(1)}, u32[]{:S(2)}, u32[]{:S(2)}) %all-to-all-start) | async-done | bytes 184352 | tf_op jit(solution)/shard_map/all_to_all | solution.py:244
  66.5 1.1 reshape.423
  68.4 3.1 reverse.1
  71.5 1.0 multiply_bitcast_fusion.1
  73.2 2.4 slice.130
  77.0 179.3 %legendre_sweep.1 = (f32[2,2,16,640]{3,2,1,0:T(8,128)}, f32[2,2,16,640]{3,2,1,0:T(8,128)}) custom-call(s32[41]{0:T(128)} %convert_element_type.54.resets, f32[41,16,128]{2,1,0:T(8,128)} %pad.21.table, f32[2,16,640]{2,1,0:T(8,128)} %multiply_add_fusion.log_start, f32[8,640]{1,0:T(8,128)} %jit_solution_.3.cosines, f32[2,2,2,16,640]{4,3,2,1,0:T(8,128)} %pad_maximum_fusion.1.weights), custom_call_target="tpu_custom_call" | custom-call | tf_op jit(solution)/shard_map/legendre_sweep/pallas_call | solution.py:191
  256.3 2.4 rev.11
  258.7 1.7 add_bitcast_fusion
  260.3 2.4 reverse.2
  263.6 1.1 all_to_all.29
  264.8 8.7 %all_to_all.35 = f32[40,4,288]{2,0,1:T(8,128)} all-to-all(f32[40,4,288]{2,0,1:T(8,128)S(1)} %copy.90), channel_id=1, replica_groups=mesh['lon'=8,'lat'=4] {'lat'}, dimensions={1} | all-to-all | bytes 368640 | tf_op jit(solution)/shard_map/all_to_all | solution.py:248
  273.6 25.1 %all-gather.2.cloned.1.call-done = f32[1280,288]{1,0:T(8,128)} async-done(((f32[160,288]{1,0:T(8,128)}), f32[1280,288]{1,0:T(8,128)}) %all-gather.2.cloned.1.call-update) | async-done | bytes 1474576 | tf_op jit(solution)/shard_map/all_gather | solution.py:249
  298.7 4.4 %convolution_bitcast_fusion = f32[1,288,512]{2,1,0:T(8,128)} fusion(f32[1280,288]{1,0:T(8,128)} %all-gather.2.cloned.1.call-done, f32[1280,512]{1,0:T(8,128)S(1)} %reshape.422), kind=kOutput, calls=%fused_computation.3 | convolution fusion | flops 1132462080 | bytes 4685824 | tf_op jit(solution)/shard_map/dot_general | solution.py:250
  (50 shorter events, 17.7 us)
Async XLA Ops:
  6.5 8.0 %copy-start = (f32[1,288,512]{2,1,0:T(8,128)S(1)}, f32[1,288,512]{2,1,0:T(8,128)}, u32[]{:S(2)}) copy-start(f32[1,288,512]{2,1,0:T(8,128)} %param.11) | copy-start | bytes 1769476
  6.5 50.1 %reduce-scatter.2.cloned.1.call-start = ((), (), s32[]{:S(2)}) async-start(), calls=%async_computation.3 | async-start | bytes 2211840 | tf_op jit(solution)/shard_map/reduce_scatter | solution.py:243
  18.0 0.7 copy-start.3
  18.0 8.5 %copy-start.5 = (s32[16]{0:T(128)S(1)}, s32[16]{0:T(128)}, u32[]{:S(2)}) copy-start(s32[16]{0:T(128)} %constant.128.clone) | copy-start | bytes 196
  31.0 7.0 %copy-start.2 = (f32[640]{0:T(1024)S(1)}, f32[640]{0:T(1024)}, u32[]{:S(2)}) copy-start(f32[640]{0:T(1024)} %constant.129.clone) | copy-start | bytes 7684
  33.3 27.1 %copy-start.1 = (f32[576]{0:T(1024)S(1)}, f32[576]{0:T(1024)}, u32[]{:S(2)}) copy-start(f32[576]{0:T(1024)} %constant.131.clone) | copy-start | bytes 6916
  56.6 9.1 %all-to-all-start = ((f32[4,40,288]{2,1,0:T(8,128)}), f32[4,40,288]{2,1,0:T(8,128)S(1)}, u32[]{:S(2)}, u32[]{:S(2)}) async-start(f32[4,40,288]{2,1,0:T(8,128)} %bitcast.49), calls=%async_computation.1 | async-start | bytes 491520 | tf_op jit(solution)/shard_map/all_to_all | solution.py:244
  60.5 238.2 %all-gather.2.cloned.1.call-start = ((), (), s32[]{:S(2)}) async-start(), calls=%async_computation.4 | async-start | bytes 2211840 | tf_op jit(solution)/shard_map/all_gather | solution.py:249
  67.7 8.7 %copy-start.4 = (f32[640]{0:T(1024)S(1)}, f32[640]{0:T(1024)}, u32[]{:S(2)}) copy-start(f32[640]{0:T(1024)} %constant.132.clone) | copy-start | bytes 7684
Sparse Core Ops, SparseCore 0:
  18.2 38.4 reduce-scatter.1
  273.7 24.9 all-gather.1

commit v2 on v1

v2 whole, which is shorter than its diff:
```python
import functools
import math

import jax
import jax.numpy as jnp
import numpy as np
from jax import lax
from jax.experimental import pallas as pl
from jax.experimental.pallas import tpu as pltpu
from jax.sharding import PartitionSpec as P

STEPS = 16
LANES = 128
RESCALE = 2.0 ** -64
THRESHOLD = 2.0 ** 32
high = lax.Precision.HIGH


def mode_order(modes, devices):
    count = modes // devices
    order = np.zeros((devices, count), np.int64)
    device = np.arange(devices)
    for slot in range((count + 1) // 2):
        order[:, slot] = slot * devices + device
        if slot != count - 1 - slot:
            order[:, count - 1 - slot] = modes - 1 - order[:, slot]
    return order


exact = lax.Precision.HIGHEST


def dot(left, right):
    return jnp.dot(left, right, precision=exact, preferred_element_type=jnp.float32)


def sweep_kernel(modes, devices, slots, where, answers, second_answers, log_start, grid,
                 gains, columns, out, earlier, latest, log_scale, weights, current_weights,
                 first_sums, sums, ladder, partial, mirror):
    blocks = second_answers.shape[0]
    padded_chains, padded_half = latest.shape
    chains = (slots + 1) // 2
    groups = padded_chains // 8
    half = columns.shape[1] // 2
    south_start = columns.shape[1] - padded_half
    device = where[0]

    shape = (4 * padded_chains, columns.shape[0])
    row = lax.broadcasted_iota(jnp.int32, shape, 0)
    column = lax.broadcasted_iota(jnp.int32, shape, 1)
    chain = row % padded_chains
    part = (row // padded_chains) % 2
    second_side = row // (2 * padded_chains)
    slot = jnp.where(second_side == 1, slots - 1 - chain, chain)
    valid = jnp.logical_and(chain < chains, jnp.logical_or(second_side == 0, slot >= chains))
    select = jnp.where(
        jnp.logical_and(valid, column == part * slots + slot), 1.0, 0.0
    ).astype(jnp.float32)
    square = (padded_half, padded_half)
    mirror[...] = jnp.where(
        lax.broadcasted_iota(jnp.int32, square, 0) + lax.broadcasted_iota(jnp.int32, square, 1)
        == padded_half - 1, 1.0, 0.0,
    ).astype(jnp.float32)
    gain = gains[...] * grid[1:2, :]
    north = dot(select, columns[:, :padded_half])
    south = dot(dot(select, columns[:, south_start:]), mirror[...])
    weights[0] = (north + south) * gain
    weights[1] = (north - south) * gain

    earlier[...] = jnp.zeros_like(earlier)
    latest[...] = jnp.zeros_like(latest)
    log_scale[...] = log_start[0]
    current_weights[...] = weights[:, :2 * padded_chains, :]
    sums[...] = jnp.zeros_like(sums)
    first_sums[...] = jnp.zeros_like(first_sums)
    ones = jnp.ones((2 * LANES, LANES), jnp.bfloat16)
    top_switch = (modes - device + STEPS - 1) // STEPS
    stride = devices // STEPS

    def one_block(block, carry):
        behind = top_switch - block
        any_reset = jnp.logical_and(
            behind >= 0, jnp.logical_and(behind % stride == 0, behind < padded_chains * stride)
        )

        @pl.when(any_reset)
        def _():
            shape = (padded_chains, padded_half)
            chain = lax.broadcasted_iota(jnp.int32, shape, 0)
            switching = jnp.where(chain < chains, chain, 0) * stride == behind
            earlier[...] = jnp.where(switching, 0.0, earlier[...])
            latest[...] = jnp.where(switching, 0.0, latest[...])
            log_scale[...] = jnp.where(switching, log_start[1], log_scale[...])
            for parity in range(2):
                for part in range(2):
                    rows = pl.ds(part * padded_chains, padded_chains)
                    later = pl.ds((2 + part) * padded_chains, padded_chains)
                    current_weights[parity, rows, :] = jnp.where(
                        switching, weights[parity, later, :], current_weights[parity, rows, :]
                    )
                    held = sums[parity, rows, :]
                    first_sums[parity, rows, :] = jnp.where(
                        switching, held, first_sums[parity, rows, :]
                    )
                    sums[parity, rows, :] = jnp.where(switching, 0.0, held)

        x = grid[0:1, :]
        reduced = []
        for group in range(groups):
            rows = pl.ds(group * 8, 8)
            tile = (8, LANES)
            chain = lax.broadcasted_iota(jnp.int32, tile, 0) + group * 8
            chain = jnp.where(chain < chains, chain, 0)
            lane = lax.broadcasted_iota(jnp.int32, tile, 1)
            first = chain * devices + device
            switch = top_switch - chain * stride
            is_first = block < switch
            order = jnp.where(is_first, first, modes - 1 - first)
            step = jnp.where(is_first, block, block - switch) * STEPS + lane
            started = step > 0
            n = order.astype(jnp.float32)
            k = jnp.maximum(step, 1).astype(jnp.float32)
            degree = n + k
            lower = degree - 1.0
            growths = jnp.where(started, jnp.sqrt(
                (4.0 * degree * degree - 1.0) / (k * (degree + n))), 0.0)
            ratios = growths * jnp.sqrt(jnp.where(
                started, (k - 1.0) * (lower + n) / jnp.maximum(4.0 * lower * lower - 1.0, 1.0), 0.0))
            starts = jnp.where(step == 0, 1.0, 0.0)[:, 0:1]
            replies = jnp.where(
                is_first,
                answers[pl.ds(block + group * 8 * stride, 8, stride=stride), :],
                jnp.broadcast_to(second_answers[pl.ds(block, 1), :], tile),
            )
            before = earlier[rows, :]
            last = latest[rows, :]
            scale = log_scale[rows, :]
            factor = jnp.exp(scale)
            for step in range(STEPS):
                current = growths[:, step:step + 1] * (x * last) - ratios[:, step:step + 1] * before
                if step == 0:
                    current = current + starts
                before, last = last, current
                legendre = current * factor
                ladder[group, step] = legendre
                reply = replies[:, step:step + 1]
                for part in range(2):
                    held = current_weights[step % 2, pl.ds(part * padded_chains + group * 8, 8), :]
                    total = None
                    for lanes in range(0, padded_half, LANES):
                        term = legendre[:, lanes:lanes + LANES] * held[:, lanes:lanes + LANES]
                        total = term if total is None else total + term
                    partial[group, pl.ds((part * STEPS + step) * 8, 8), :] = total * reply
            large = jnp.maximum(jnp.abs(before), jnp.abs(last)) > THRESHOLD
            shrink = jnp.where(large, RESCALE, 1.0)
            earlier[rows, :] = before * shrink
            latest[rows, :] = last * shrink
            log_scale[rows, :] = scale + jnp.where(large, 64.0 * math.log(2.0), 0.0)
            value = partial[group]
            upper = value.astype(jnp.bfloat16)
            rest = (value - upper.astype(jnp.float32)).astype(jnp.bfloat16)
            reduced.append(jnp.dot(
                jnp.concatenate([upper, rest], axis=1), ones,
                preferred_element_type=jnp.float32,
            ))
        for group in range(groups):
            partial[group] = reduced[group]
        for group in range(groups):
            for lanes in range(0, padded_half, LANES):
                totals = [[None, None], [None, None]]
                for step in range(STEPS):
                    legendre = ladder[group, step, :, pl.ds(lanes, LANES)]
                    for part in range(2):
                        term = legendre * partial[group, pl.ds((part * STEPS + step) * 8, 8), :]
                        total = totals[step % 2][part]
                        totals[step % 2][part] = term if total is None else total + term
                for parity in range(2):
                    for part in range(2):
                        rows = pl.ds(part * padded_chains + group * 8, 8)
                        sums[parity, rows, pl.ds(lanes, LANES)] += totals[parity][part]
        return carry

    lax.fori_loop(0, blocks, one_block, 0)
    both = [jnp.concatenate([first_sums[p], sums[p]], axis=0) for p in range(2)]
    shape = (columns.shape[0], 4 * padded_chains)
    row = lax.broadcasted_iota(jnp.int32, shape, 0)
    column = lax.broadcasted_iota(jnp.int32, shape, 1)
    part, slot = row // slots, row % slots
    side = jnp.where(slot < chains, 0, 1)
    chain = jnp.where(slot < chains, slot, slots - 1 - slot)
    back = jnp.where(
        column == (side * 2 + part) * padded_chains + chain, 1.0, 0.0
    ).astype(jnp.float32)
    north = dot(back, both[0] + both[1])
    south = dot(dot(back, both[0] - both[1]), mirror[...])
    out[:, :south_start] = north[:, :south_start]
    overlap = padded_half - south_start
    lane = lax.broadcasted_iota(jnp.int32, (columns.shape[0], overlap), 1) + south_start
    out[:, south_start:padded_half] = jnp.where(
        lane < half, north[:, south_start:], south[:, :overlap]
    )
    out[:, padded_half:] = south[:, overlap:]


def sweep(columns, response, device, devices, modes, cells):
    rows = columns.shape[1]
    slots = columns.shape[0] // 2
    half = rows // 2
    padded_half = -(-half // LANES) * LANES
    chains = (slots + 1) // 2
    padded_chains = -(-chains // 8) * 8
    blocks = modes // STEPS + 1
    total_steps = blocks * STEPS

    lanes = ((0, 0), (0, LANES - STEPS))
    count = blocks + padded_chains * devices // STEPS
    padded_response = jnp.pad(response, (STEPS, (count + 2) * STEPS + devices))
    answers = lax.dynamic_slice_in_dim(padded_response, STEPS + device, count * STEPS)
    offset = modes - 1 - device - ((modes - device + STEPS - 1) // STEPS) * STEPS
    second_answers = lax.dynamic_slice_in_dim(padded_response, STEPS + offset, total_steps)
    answers = jnp.pad(answers.reshape(count, STEPS), lanes)
    second_answers = jnp.pad(second_answers.reshape(blocks, STEPS), lanes)

    inside = np.arange(padded_half) < half
    colatitude = (np.arange(padded_half) + 0.5) * (math.pi / rows)
    colatitude = np.where(inside, colatitude, math.pi / 2)
    area = np.sin(colatitude) * (math.pi / rows) * (2.0 * math.pi / cells)
    grid = np.zeros((8, padded_half), np.float32)
    grid[0] = np.cos(colatitude)
    grid[1] = np.where(inside, area, 0.0)
    log_sines = jnp.asarray(np.log(np.sin(colatitude)).astype(np.float32))
    log_norm = np.array([
        0.5 * (math.lgamma(m + 1.5) - math.lgamma(1.5) - math.lgamma(m + 1.0))
        - 0.5 * math.log(4.0 * math.pi)
        for m in range(modes)
    ])
    chain = np.where(np.arange(padded_chains) < chains, np.arange(padded_chains), 0)
    first = np.arange(devices)[:, None] + chain * devices
    orders = np.stack([first, modes - 1 - first], axis=1)
    packed = np.stack([log_norm[orders], orders, np.where(orders == 0, 1.0, 2.0)], axis=1)
    packed = lax.dynamic_index_in_dim(
        jnp.asarray(packed.astype(np.float32)), device, 0, keepdims=False
    )
    log_start = packed[0][:, :, None] + packed[1][:, :, None] * log_sines
    gains = jnp.broadcast_to(packed[2][:, None, :], (2, 2, padded_chains))
    gains = gains.reshape(4 * padded_chains, 1)

    vmem = pl.BlockSpec(memory_space=pltpu.VMEM)
    state = pltpu.VMEM((padded_chains, padded_half), jnp.float32)
    pair = pltpu.VMEM((2, 2 * padded_chains, padded_half), jnp.float32)
    groups = padded_chains // 8
    return pl.pallas_call(
        functools.partial(sweep_kernel, modes, devices, slots),
        out_shape=jax.ShapeDtypeStruct(columns.shape, jnp.float32),
        in_specs=[pl.BlockSpec(memory_space=pltpu.SMEM)] + [vmem] * 6,
        out_specs=vmem,
        scratch_shapes=[
            state, state, state,
            pltpu.VMEM((2, 4 * padded_chains, padded_half), jnp.float32),
            pair, pair, pair,
            pltpu.VMEM((groups, STEPS, 8, padded_half), jnp.float32),
            pltpu.VMEM((groups, 2 * STEPS * 8, LANES), jnp.float32),
            pltpu.VMEM((padded_half, padded_half), jnp.float32),
        ],
        name="legendre_sweep",
    )(device.reshape(1), answers, second_answers, log_start, jnp.asarray(grid), gains, columns)


def shards(modes, height, response):
    fields, band_rows, lon_cells = height.shape
    lon_count = lax.axis_size("lon")
    lat_count = lax.axis_size("lat")
    lon_index = lax.axis_index("lon")
    lat_index = lax.axis_index("lat")
    devices = lon_count * lat_count
    cells = lon_count * lon_cells
    device = lon_index * lat_count + lat_index

    order = mode_order(modes, devices)
    local = np.arange(lon_cells)
    angles = (order[:, :, None] * local % cells) * (2.0 * math.pi / cells)
    cos_table = jnp.asarray(np.cos(angles).astype(np.float32))
    sin_table = jnp.asarray(np.sin(angles).astype(np.float32))
    turn = (jnp.asarray(order.astype(np.int32)) * (lon_index * lon_cells) % cells)
    turn = turn.astype(jnp.float32)[:, :, None] * (2.0 * math.pi / cells)
    cos_turn, sin_turn = jnp.cos(turn), jnp.sin(turn)
    table = jnp.stack(
        [
            cos_turn * cos_table - sin_turn * sin_table,
            -(sin_turn * cos_table + cos_turn * sin_table),
        ],
        axis=1,
    ).reshape(2 * modes, lon_cells)

    outputs = []
    for field in range(fields):
        partial = lax.dot_general(
            table, height[field], (((1,), (1,)), ((), ())), precision=high,
            preferred_element_type=jnp.float32,
        )
        spectrum = lax.psum_scatter(partial, "lon", scatter_dimension=0, tiled=True)
        columns = lax.all_to_all(spectrum, "lat", split_axis=0, concat_axis=1, tiled=True)
        synthesis = sweep(columns, response, device, devices, modes, cells)
        bands = lax.all_to_all(synthesis, "lat", split_axis=1, concat_axis=0, tiled=True)
        gathered = lax.all_gather(bands, "lon", axis=0, tiled=True)
        outputs.append(lax.dot_general(
            gathered, table, (((0,), (0,)), ((), ())), precision=high,
            preferred_element_type=jnp.float32,
        ))
    return jnp.stack(outputs)


def solution(mesh):
    placed = (P(None, "lat", "lon"), P())

    def loading(height, response):
        body = functools.partial(shards, response.shape[0])
        return jax.shard_map(
            body, mesh=mesh, in_specs=placed, out_specs=P(None, "lat", "lon"), check_vma=False
        )(height, response)

    return loading
```

time: 312 us -> 142 us (0.46)
  Pallas kernels: 179 us -> 26.9 us
  local copies, waits for them, and re-layouts: 31.4 us -> 9.95 us
  waiting for transfers between devices: 48.3 us -> 64.7 us
  other arithmetic: 16.8 us -> 5.97 us
    pallas_call x1, Pallas kernels: 179 us -> 26.9 us  [sweep(): pl.pallas_call(functools.partial(sweep_kernel, modes, devices, slots), ou...]
    reduce_scatter x1, waiting for transfers between devices: 17.9 us -> 35 us  [shards(): spectrum = lax.psum_scatter(partial, 'lon', scatter_dimension=0, tiled=True)]
    another operation x13 -> x0, local copies, waits for them, and re-layouts: 9.93 us -> none  [the longest x11 9.28 us: sweep(): jnp.stack([from_device[c * devices:c * devices + total_steps] for c in ch...]
    unnamed x15 -> x6, local copies, waits for them, and re-layouts: 6.24 us -> 0.65 us
    slice x3 -> x0, local copies, waits for them, and re-layouts: 3.17 us -> none  [the longest x1 2.35 us: sweep(): folded[:, :, ::-1][:, :, :chains]]
  transfers between devices with their start and end apart: 3 -> 3, of which waited for: 3 -> 3; matrix products, arithmetic and copies ran while one was open for 6% -> 3% of each run, Pallas kernels for 0% -> 0%
where the time goes in v2:
time: 142 us
  waiting for transfers between devices  64.7 us (46%)
  Pallas kernels  26.9 us (19%)
  between operations  13.5 us (10%)
  local copies, waits for them, and re-layouts  9.95 us (7%)
  blocking collectives  8.73 us (6%)
  matrix products  7.92 us (6%)
  other arithmetic  5.97 us (4%)
  starting transfers between devices  3.85 us (3%)
    reduce_scatter x1, waiting for transfers between devices, shards(): spectrum = lax.psum_scatter(partial, 'lon', scatter_dimension=0, tiled=True)  35 us
    pallas_call x1, Pallas kernels, sweep(): pl.pallas_call(functools.partial(sweep_kernel, modes, devices, slots), ou...  26.9 us
    all_gather x1, waiting for transfers between devices, shards(): gathered = lax.all_gather(bands, 'lon', axis=0, tiled=True)  25.1 us
    all_to_all x1, blocking collectives, shards(): lax.all_to_all(synthesis, 'lat', split_axis=1, concat_axis=0, tiled=True)  8.73 us
    all_to_all x1, waiting for transfers between devices, shards(): lax.all_to_all(spectrum, 'lat', split_axis=0, concat_axis=1, tiled=True)  4.61 us
    dot_general x1, matrix products, shards(): lax.dot_general(gathered, table, (((0,), (0,)), ((), ())), precision=high...  4.43 us
    another operation x2, other arithmetic, shards(): jnp.stack([cos_turn * cos_table - sin_turn * sin_table, -(sin_turn * cos_...  4.4 us
    all_to_all x1, starting transfers between devices, shards(): lax.all_to_all(spectrum, 'lat', split_axis=0, concat_axis=1, tiled=True)  3.85 us
  transfers between devices with their start and end apart: 3, of which 3 were waited for; matrix products, arithmetic and copies ran while one was open for 3% of the time, Pallas kernels for 0%

profile of v2, /device:TPU:0, one launch (start us, length us, event | category | flops | bytes accessed | tf_op | source)
XLA Modules:
  0.0 141.5 jit_solution(18115980239806444797)
XLA Ops:
  6.5 0.9 fusion.6
  7.4 2.3 %subtract_bitcast_fusion = (f32[32,1,20,512]{3,2,1,0:T(8,128)S(1)}, f32[32,1,20,512]{3,2,1,0:T(8,128)S(1)}) fusion(f32[32,20,512]{2,1,0:T(8,128)} %constant.78.clone, f32[32,20,512]{2,1,0:T(8,128)} %constant.77.clone, f32[32,20]{1,0:T(8,128)S(1)} %get-tuple-element.11, f32[32,20]{1,0:T(8,128)S(1)} %get-tuple-element.10), kind=kLoop, calls=%fused_computation.2 | loop fusion | flops 2293760 | bytes 5248000 | tf_op jit(solution)/shard_map/stack | solution.py:287
  9.7 2.1 %pad_maximum_fusion = f32[32,2,20,512]{3,2,1,0:T(8,128)} fusion(f32[32,1,20,512]{3,2,1,0:T(8,128)S(1)} %get-tuple-element.6, f32[32,1,20,512]{3,2,1,0:T(8,128)S(1)} %get-tuple-element.5), kind=kLoop, calls=%fused_computation | loop fusion | flops 655360 | bytes 5242880 | tf_op jit(solution)/shard_map/stack | solution.py:287
  11.8 2.7 %reshape.40 = f32[1280,512]{1,0:T(8,128)S(1)} reshape(f32[32,2,20,512]{3,2,1,0:T(8,128)} %pad_maximum_fusion) | data formatting | bytes 5242880 | tf_op jit(solution)/shard_map/reshape | solution.py:293
  14.5 3.5 %fusion = f32[1280,288]{1,0:T(8,128)} fusion(f32[1280,512]{1,0:T(8,128)S(1)} %reshape.40, f32[1,288,512]{2,1,0:T(8,128)S(1)} %copy-done), kind=kOutput, calls=%fused_computation.4 | convolution fusion | flops 1132462080 | bytes 4685824 | tf_op jit(solution)/shard_map/dot_general | solution.py:297
  18.0 0.6 copy-done.1
  18.7 0.1 pad_dynamic-slice_fusion
  18.8 0.7 dynamic-slice_bitcast_fusion
  19.5 0.7 reshape.41.gains
  20.2 0.1 pad_dynamic-slice_fusion.1
  20.3 0.1 reshape.37
  20.4 0.6 pad.14.second_answers
  21.0 0.6 pad.13.answers
  21.6 35.0 %reduce-scatter.2.cloned.1.call-done = f32[160,288]{1,0:T(8,128)} async-done(((f32[1280,288]{1,0:T(8,128)}), f32[160,288]{1,0:T(8,128)}) %reduce-scatter.2.cloned.1.call-update) | async-done | bytes 184336 | tf_op jit(solution)/shard_map/reduce_scatter | solution.py:301
  56.6 3.8 %all-to-all-start = ((f32[4,40,288]{2,1,0:T(8,128)}), f32[4,40,288]{2,1,0:T(8,128)S(1)}, u32[]{:S(2)}, u32[]{:S(2)}) async-start(f32[4,40,288]{2,1,0:T(8,128)} %bitcast.28), calls=%async_computation.1 | async-start | bytes 491520 | tf_op jit(solution)/shard_map/all_to_all | solution.py:302
  60.4 0.7 multiply_add_fusion.log_start
  61.2 4.6 %all-to-all-done = f32[4,40,288]{2,1,0:T(8,128)S(1)} async-done(((f32[4,40,288]{2,1,0:T(8,128)}), f32[4,40,288]{2,1,0:T(8,128)S(1)}, u32[]{:S(2)}, u32[]{:S(2)}) %all-to-all-start) | async-done | bytes 184352 | tf_op jit(solution)/shard_map/all_to_all | solution.py:302
  65.8 0.8 copy.16
  66.5 1.8 %all_to_all.31.columns = f32[40,1152]{1,0:T(8,128)} reshape(f32[40,4,288]{2,1,0:T(4,128)} %copy.16) | data formatting | bytes 368640 | tf_op jit(solution)/shard_map/all_to_all | solution.py:302
  68.3 26.9 %legendre_sweep.1 = f32[40,1152]{1,0:T(8,128)} custom-call(s32[1]{0:T(128)} %bitcast.where, f32[73,128]{1,0:T(8,128)} %pad.13.answers, f32[41,128]{1,0:T(8,128)} %pad.14.second_answers, f32[2,16,640]{2,1,0:T(8,128)} %multiply_add_fusion.log_start, f32[8,640]{1,0:T(8,128)} %constant.82.clone.grid, f32[64,1]{1,0:T(8,128)} %reshape.41.gains, ...), custom_call_target="tpu_custom_call" | custom-call | tf_op jit(solution)/shard_map/legendre_sweep/pallas_call | solution.py:252
  95.2 1.1 all_to_all.32
  96.4 8.7 %all_to_all.38 = f32[40,4,288]{2,0,1:T(8,128)} all-to-all(f32[40,4,288]{2,0,1:T(8,128)S(1)} %copy.18), channel_id=1, replica_groups=mesh['lon'=8,'lat'=4] {'lat'}, dimensions={1} | all-to-all | bytes 368640 | tf_op jit(solution)/shard_map/all_to_all | solution.py:304
  105.1 25.1 %all-gather.2.cloned.1.call-done = f32[1280,288]{1,0:T(8,128)} async-done(((f32[160,288]{1,0:T(8,128)}), f32[1280,288]{1,0:T(8,128)}) %all-gather.2.cloned.1.call-update) | async-done | bytes 1474576 | tf_op jit(solution)/shard_map/all_gather | solution.py:305
  130.3 4.4 %convolution_bitcast_fusion = f32[1,288,512]{2,1,0:T(8,128)} fusion(f32[1280,288]{1,0:T(8,128)} %all-gather.2.cloned.1.call-done, f32[1280,512]{1,0:T(8,128)S(1)} %reshape.40), kind=kOutput, calls=%fused_computation.3 | convolution fusion | flops 1132462080 | bytes 4685824 | tf_op jit(solution)/shard_map/dot_general | solution.py:306
  (12 shorter events, 0.1 us)
Async XLA Ops:
  6.5 7.9 %copy-start = (f32[1,288,512]{2,1,0:T(8,128)S(1)}, f32[1,288,512]{2,1,0:T(8,128)}, u32[]{:S(2)}) copy-start(f32[1,288,512]{2,1,0:T(8,128)} %param.8) | copy-start | bytes 1769476
  6.5 50.1 %reduce-scatter.2.cloned.1.call-start = ((), (), s32[]{:S(2)}) async-start(), calls=%async_computation.3 | async-start | bytes 2211840 | tf_op jit(solution)/shard_map/reduce_scatter | solution.py:301
  18.0 0.7 copy-start.1
  18.0 42.5 %copy-start.2 = (f32[640]{0:T(1024)S(1)}, f32[640]{0:T(1024)}, u32[]{:S(2)}) copy-start(f32[640]{0:T(1024)} %constant.80.clone) | copy-start | bytes 7684
  56.6 9.2 %all-to-all-start = ((f32[4,40,288]{2,1,0:T(8,128)}), f32[4,40,288]{2,1,0:T(8,128)S(1)}, u32[]{:S(2)}, u32[]{:S(2)}) async-start(f32[4,40,288]{2,1,0:T(8,128)} %bitcast.28), calls=%async_computation.1 | async-start | bytes 491520 | tf_op jit(solution)/shard_map/all_to_all | solution.py:302
  60.4 69.8 %all-gather.2.cloned.1.call-start = ((), (), s32[]{:S(2)}) async-start(), calls=%async_computation.4 | async-start | bytes 2211840 | tf_op jit(solution)/shard_map/all_gather | solution.py:305
Sparse Core Ops, SparseCore 0:
  18.1 38.4 reduce-scatter.1
  105.3 24.9 all-gather.1

commit v3 on v2

--- a/solution.py
+++ b/solution.py
@@ -266,6 +266,59 @@
     )(device.reshape(1), answers, second_answers, log_start, jnp.asarray(grid), gains, columns)
 
 
+def gather_kernel(count, block_ref, out_ref, send, receive):
+    me = lax.axis_index("lon")
+    core, chip, chips = me % 2, me // 2, count // 2
+    partner = chip * 2 + 1 - core
+    rows = block_ref.shape[0]
+    peers = [((chip + k) % chips) * 2 + core for k in range(1, chips)]
+    barrier = pltpu.get_barrier_semaphore()
+    for peer in peers + [partner]:
+        pl.semaphore_signal(
+            barrier, inc=1, device_id={"lon": peer}, device_id_type=pl.DeviceIdType.MESH
+        )
+    pl.semaphore_wait(barrier, chips)
+
+    def push(source, owner, target, index):
+        copy = pltpu.make_async_remote_copy(
+            src_ref=source,
+            dst_ref=out_ref.at[pl.ds(pl.multiple_of(owner * rows, 8), rows)],
+            send_sem=send.at[index],
+            recv_sem=receive.at[index],
+            device_id={"lon": target},
+            device_id_type=pl.DeviceIdType.MESH,
+        )
+        copy.start()
+        return copy
+
+    copies = [push(block_ref, me, peer, k) for k, peer in enumerate(peers)]
+    shared = [push(block_ref, me, partner, chips - 1)]
+    out_ref[pl.ds(pl.multiple_of(me * rows, 8), rows), :] = block_ref[...]
+    for k in list(range(0, chips - 1, 2)) + list(range(1, chips - 1, 2)):
+        copies[k].wait_recv()
+        owner = ((chip + chips - 1 - k) % chips) * 2 + core
+        arrived = out_ref.at[pl.ds(pl.multiple_of(owner * rows, 8), rows)]
+        shared.append(push(arrived, owner, partner, chips + k))
+    for copy in copies:
+        copy.wait_send()
+    for copy in shared:
+        copy.wait()
+
+
+def gather(block, count):
+    vmem = pl.BlockSpec(memory_space=pltpu.VMEM)
+    copies = count - 1
+    return pl.pallas_call(
+        functools.partial(gather_kernel, count),
+        out_shape=jax.ShapeDtypeStruct((count * block.shape[0], block.shape[1]), block.dtype),
+        in_specs=[vmem],
+        out_specs=vmem,
+        scratch_shapes=[pltpu.SemaphoreType.DMA((copies,)), pltpu.SemaphoreType.DMA((copies,))],
+        compiler_params=pltpu.CompilerParams(collective_id=0, has_side_effects=True),
+        name="gather_bands",
+    )(block)
+
+
 def shards(modes, height, response):
     fields, band_rows, lon_cells = height.shape
     lon_count = lax.axis_size("lon")
@@ -302,7 +355,7 @@
         columns = lax.all_to_all(spectrum, "lat", split_axis=0, concat_axis=1, tiled=True)
         synthesis = sweep(columns, response, device, devices, modes, cells)
         bands = lax.all_to_all(synthesis, "lat", split_axis=1, concat_axis=0, tiled=True)
-        gathered = lax.all_gather(bands, "lon", axis=0, tiled=True)
+        gathered = gather(bands, lon_count)
         outputs.append(lax.dot_general(
             gathered, table, (((0,), (0,)), ((), ())), precision=high,
             preferred_element_type=jnp.float32,

time: 142 us -> 141 us (level); the launches traced: 142 us -> 138 us
  waiting for transfers between devices: 64.7 us -> 39.7 us
  Pallas kernels: 26.9 us -> 48.6 us
    all_gather x1 -> x0, waiting for transfers between devices: 25.1 us -> none  [shards(): gathered = lax.all_gather(bands, 'lon', axis=0, tiled=True)]
    pallas_call x0 -> x1, Pallas kernels: none -> 21.7 us  [gather(): pl.pallas_call(functools.partial(gather_kernel, count), out_shape=jax.Sha...]
  transfers between devices with their start and end apart: 3 -> 2, of which waited for: 3 -> 2; matrix products, arithmetic and copies ran while one was open for 3% -> 3% of each run, Pallas kernels for 0% -> 0%
where the time goes in v3:
time: 141 us; the launch traced here: 138 us
  Pallas kernels  48.6 us (34%)
  waiting for transfers between devices  39.7 us (28%)
  between operations  13.5 us (10%)
  local copies, waits for them, and re-layouts  9.94 us (7%)
  blocking collectives  8.75 us (6%)
  matrix products  7.93 us (6%)
  other arithmetic  5.98 us (4%)
  starting transfers between devices  3.71 us (3%)
    reduce_scatter x1, waiting for transfers between devices, shards(): spectrum = lax.psum_scatter(partial, 'lon', scatter_dimension=0, tiled=True)  35.1 us
    pallas_call x1, Pallas kernels, sweep(): pl.pallas_call(functools.partial(sweep_kernel, modes, devices, slots), ou...  26.9 us
    pallas_call x1, Pallas kernels, gather(): pl.pallas_call(functools.partial(gather_kernel, count), out_shape=jax.Sha...  21.7 us
    all_to_all x1, blocking collectives, shards(): lax.all_to_all(synthesis, 'lat', split_axis=1, concat_axis=0, tiled=True)  8.75 us
    all_to_all x1, waiting for transfers between devices, shards(): lax.all_to_all(spectrum, 'lat', split_axis=0, concat_axis=1, tiled=True)  4.62 us
    dot_general x1, matrix products, shards(): lax.dot_general(gathered, table, (((0,), (0,)), ((), ())), precision=high...  4.43 us
    another operation x2, other arithmetic, shards(): jnp.stack([cos_turn * cos_table - sin_turn * sin_table, -(sin_turn * cos_...  4.41 us
    all_to_all x1, starting transfers between devices, shards(): lax.all_to_all(spectrum, 'lat', split_axis=0, concat_axis=1, tiled=True)  3.71 us
  transfers between devices with their start and end apart: 2, of which 2 were waited for; matrix products, arithmetic and copies ran while one was open for 3% of the time, Pallas kernels for 0%

profile of v3, /device:TPU:0, one launch (start us, length us, event | category | flops | bytes accessed | tf_op | source)
XLA Modules:
  0.0 138.1 jit_solution(3286862985687278596)
XLA Ops:
  6.5 0.9 fusion.6
  7.4 2.3 %subtract_bitcast_fusion = (f32[32,1,20,512]{3,2,1,0:T(8,128)S(1)}, f32[32,1,20,512]{3,2,1,0:T(8,128)S(1)}) fusion(f32[32,20,512]{2,1,0:T(8,128)} %constant.78.clone, f32[32,20,512]{2,1,0:T(8,128)} %constant.77.clone, f32[32,20]{1,0:T(8,128)S(1)} %get-tuple-element.11, f32[32,20]{1,0:T(8,128)S(1)} %get-tuple-element.10), kind=kLoop, calls=%fused_computation.2 | loop fusion | flops 2293760 | bytes 5248000 | tf_op jit(solution)/shard_map/stack | solution.py:340
  9.7 2.1 %pad_maximum_fusion = f32[32,2,20,512]{3,2,1,0:T(8,128)} fusion(f32[32,1,20,512]{3,2,1,0:T(8,128)S(1)} %get-tuple-element.6, f32[32,1,20,512]{3,2,1,0:T(8,128)S(1)} %get-tuple-element.5), kind=kLoop, calls=%fused_computation | loop fusion | flops 655360 | bytes 5242880 | tf_op jit(solution)/shard_map/stack | solution.py:340
  11.8 2.7 %reshape.40 = f32[1280,512]{1,0:T(8,128)S(1)} reshape(f32[32,2,20,512]{3,2,1,0:T(8,128)} %pad_maximum_fusion) | data formatting | bytes 5242880 | tf_op jit(solution)/shard_map/reshape | solution.py:346
  14.5 3.5 %fusion = f32[1280,288]{1,0:T(8,128)} fusion(f32[1280,512]{1,0:T(8,128)S(1)} %reshape.40, f32[1,288,512]{2,1,0:T(8,128)S(1)} %copy-done), kind=kOutput, calls=%fused_computation.4 | convolution fusion | flops 1132462080 | bytes 4685824 | tf_op jit(solution)/shard_map/dot_general | solution.py:350
  18.0 0.6 copy-done.1
  18.7 0.1 pad_dynamic-slice_fusion
  18.8 0.7 dynamic-slice_bitcast_fusion
  19.6 0.7 reshape.41.gains
  20.3 0.1 pad_dynamic-slice_fusion.1
  20.3 0.1 reshape.37
  20.4 0.6 pad.14.second_answers
  21.0 0.6 pad.13.answers
  21.7 35.1 %reduce-scatter.2.cloned.1.call-done = f32[160,288]{1,0:T(8,128)} async-done(((f32[1280,288]{1,0:T(8,128)}), f32[160,288]{1,0:T(8,128)}) %reduce-scatter.2.cloned.1.call-update) | async-done | bytes 184336 | tf_op jit(solution)/shard_map/reduce_scatter | solution.py:354
  56.8 3.7 %all-to-all-start = ((f32[4,40,288]{2,1,0:T(8,128)}), f32[4,40,288]{2,1,0:T(8,128)S(1)}, u32[]{:S(2)}, u32[]{:S(2)}) async-start(f32[4,40,288]{2,1,0:T(8,128)} %bitcast.28), calls=%async_computation.1 | async-start | bytes 491520 | tf_op jit(solution)/shard_map/all_to_all | solution.py:355
  60.5 0.7 multiply_add_fusion.log_start
  61.2 4.6 %all-to-all-done = f32[4,40,288]{2,1,0:T(8,128)S(1)} async-done(((f32[4,40,288]{2,1,0:T(8,128)}), f32[4,40,288]{2,1,0:T(8,128)S(1)}, u32[]{:S(2)}, u32[]{:S(2)}) %all-to-all-start) | async-done | bytes 184352 | tf_op jit(solution)/shard_map/all_to_all | solution.py:355
  65.8 0.8 copy.17
  66.6 1.8 %all_to_all.31.columns = f32[40,1152]{1,0:T(8,128)} reshape(f32[40,4,288]{2,1,0:T(4,128)} %copy.17) | data formatting | bytes 368640 | tf_op jit(solution)/shard_map/all_to_all | solution.py:355
  68.3 26.9 %legendre_sweep.1 = f32[40,1152]{1,0:T(8,128)} custom-call(s32[1]{0:T(128)} %bitcast.where, f32[73,128]{1,0:T(8,128)} %pad.13.answers, f32[41,128]{1,0:T(8,128)} %pad.14.second_answers, f32[2,16,640]{2,1,0:T(8,128)} %multiply_add_fusion.log_start, f32[8,640]{1,0:T(8,128)} %constant.82.clone.grid, f32[64,1]{1,0:T(8,128)} %reshape.41.gains, ...), custom_call_target="tpu_custom_call" | custom-call | tf_op jit(solution)/shard_map/legendre_sweep/pallas_call | solution.py:252
  95.2 1.1 all_to_all.32
  96.4 8.8 %all_to_all.38 = f32[40,4,288]{2,0,1:T(8,128)} all-to-all(f32[40,4,288]{2,0,1:T(8,128)S(1)} %copy.19), channel_id=1, replica_groups=mesh['lon'=8,'lat'=4] {'lat'}, dimensions={1} | all-to-all | bytes 368640 | tf_op jit(solution)/shard_map/all_to_all | solution.py:357
  105.2 21.7 %gather_bands.1 = f32[1280,288]{1,0:T(8,128)} custom-call(f32[160,288]{1,0:T(8,128)} %bitcast.27), custom_call_target="tpu_custom_call" | custom-call | tf_op jit(solution)/shard_map/gather_bands/pallas_call | solution.py:311
  126.8 4.4 %convolution_bitcast_fusion = f32[1,288,512]{2,1,0:T(8,128)} fusion(f32[1280,288]{1,0:T(8,128)} %gather_bands.1, f32[1280,512]{1,0:T(8,128)S(1)} %reshape.40), kind=kOutput, calls=%fused_computation.3 | convolution fusion | flops 1132462080 | bytes 4685824 | tf_op jit(solution)/shard_map/dot_general | solution.py:359
  (10 shorter events, 0.1 us)
Async XLA Ops:
  6.5 8.0 %copy-start = (f32[1,288,512]{2,1,0:T(8,128)S(1)}, f32[1,288,512]{2,1,0:T(8,128)}, u32[]{:S(2)}) copy-start(f32[1,288,512]{2,1,0:T(8,128)} %param.8) | copy-start | bytes 1769476
  6.5 50.2 %reduce-scatter.2.cloned.1.call-start = ((), (), s32[]{:S(2)}) async-start(), calls=%async_computation.3 | async-start | bytes 2211840 | tf_op jit(solution)/shard_map/reduce_scatter | solution.py:354
  18.0 0.7 copy-start.1
  18.0 42.5 %copy-start.2 = (f32[640]{0:T(1024)S(1)}, f32[640]{0:T(1024)}, u32[]{:S(2)}) copy-start(f32[640]{0:T(1024)} %constant.80.clone) | copy-start | bytes 7684
  56.8 9.0 %all-to-all-start = ((f32[4,40,288]{2,1,0:T(8,128)}), f32[4,40,288]{2,1,0:T(8,128)S(1)}, u32[]{:S(2)}, u32[]{:S(2)}) async-start(f32[4,40,288]{2,1,0:T(8,128)} %bitcast.28), calls=%async_computation.1 | async-start | bytes 491520 | tf_op jit(solution)/shard_map/all_to_all | solution.py:355
Sparse Core Ops, SparseCore 0:
  18.2 38.5 reduce-scatter.1
